TPU v7x, 32 devices: a whole 2x2x4 slice. The times are simulated.
32 devices in a mesh: dp: 4 (over z), expert: 4 (over y, x), seq: 2 (over core).
Axes of the slice: x: 2, y: 2, z: 4, core: 2. Of those that a mesh axis runs over, the one named last changes fastest.
Arguments:
- tokens: bfloat16 [4096, 2048], P(('dp', 'expert', 'seq')), may hold values from -6 to 6
- out_grad: bfloat16 [4096, 2048], P(('dp', 'expert', 'seq')), may hold values from -6 to 6
- expert_ids: int32 [4096, 2], P(('dp', 'expert', 'seq')), may hold values from 0 to 3, all different within a row; in each aligned block of 128 rows (0 to 127, 128 to 255, ...) at most 96 rows name the same one
- gate_values: float32 [4096, 2], P(('dp', 'expert', 'seq')), may hold values from 0.2 to 1
- gate_weight: bfloat16 [4, 2048, 512], P('expert', 'dp', 'seq'), may hold values from -0.125 to 0.125
- up_weight: bfloat16 [4, 2048, 512], P('expert', 'dp', 'seq'), may hold values from -0.125 to 0.125
- down_weight: bfloat16 [4, 2048, 512], P('expert', 'dp', 'seq'), may hold values from -0.25 to 0.25
Outputs:
- in_grad: bfloat16 [4096, 2048], P(('dp', 'expert', 'seq'))
- gate_grads: float32 [4096, 2], P(('dp', 'expert', 'seq'))
- gate_weight_grad: bfloat16 [4, 2048, 512], P('expert', 'dp', 'seq')
- up_weight_grad: bfloat16 [4, 2048, 512], P('expert', 'dp', 'seq')
- down_weight_grad: bfloat16 [4, 2048, 512], P('expert', 'dp', 'seq')
Inputs may be any that keep to these rules, and one draw needn't show every extreme that they name: `expert_ids`: the two ids of a row differ. Within the 128 rows of one device no expert is named more than 96 times, a bound that some block reaches.
All inputs are finite; a program needn't handle non-finite values.
Results may differ from a plain program's by a relative error of at most 0.017.
Values may be sent and summed in bfloat16 or wider, within the bound.
No kernel may reach another device: no remote copies, remote signals or barrier semaphores. Data moves between devices by JAX's collectives and lax.ppermute only.
A program may use at most 64 MiB of HBM per device.

v0:
```python
import jax
import jax.numpy as jnp
from jax import lax
from jax.sharding import PartitionSpec as P


def route_slots(block_ids, expert_count, capacity):
    flat_ids = block_ids.reshape(-1)
    onehot = (flat_ids[:, None] == jnp.arange(expert_count, dtype=jnp.int32)[None, :]).astype(
        jnp.int32
    )
    position = jnp.sum((jnp.cumsum(onehot, axis=0) - 1) * onehot, axis=1)
    return flat_ids * capacity + position


def expert_half(routed, grads_in, gate_vals, gate_cols, up_cols, down_cols):
    contract_last = (((1,), (1,)), ((), ()))
    gate_pre = jnp.dot(routed, gate_cols, preferred_element_type=jnp.float32)
    up_pre = jnp.dot(routed, up_cols, preferred_element_type=jnp.float32)
    sigmoid_val = jax.nn.sigmoid(gate_pre)
    activated = gate_pre * sigmoid_val
    hidden = (activated * up_pre).astype(jnp.bfloat16)
    produced = lax.dot_general(hidden, down_cols, contract_last, preferred_element_type=jnp.float32)
    gate_inner = jnp.sum(grads_in.astype(jnp.float32) * produced, axis=1)
    scaled = (gate_vals[:, None] * grads_in.astype(jnp.float32)).astype(jnp.bfloat16)
    hidden_grad = jnp.dot(scaled, down_cols, preferred_element_type=jnp.float32)
    gate_grad = (
        hidden_grad * up_pre * sigmoid_val * (1.0 + gate_pre * (1.0 - sigmoid_val))
    ).astype(jnp.bfloat16)
    up_grad = (hidden_grad * activated).astype(jnp.bfloat16)
    back_sum = lax.dot_general(
        gate_grad, gate_cols, contract_last, preferred_element_type=jnp.float32
    )
    back_sum = back_sum + lax.dot_general(
        up_grad, up_cols, contract_last, preferred_element_type=jnp.float32
    )
    return (hidden, scaled, gate_grad, up_grad, back_sum.astype(jnp.bfloat16), gate_inner)


def per_device(tokens, out_grad, expert_ids, gate_values, gate_weight, up_weight, down_weight):
    tok_count, model_width = tokens.shape
    expert_span = lax.axis_size("expert")
    seq_count = lax.axis_size("seq")
    expert_count = expert_span * gate_weight.shape[0]
    capacity = min(tok_count, 3 * tok_count // expert_span)
    half_width = gate_weight.shape[2]
    slot_index = route_slots(expert_ids, expert_count, capacity)
    pair_ids = jnp.arange(2 * tok_count, dtype=jnp.int32)
    sources = (
        jnp.full((expert_count * capacity,), 2 * tok_count, jnp.int32).at[slot_index].set(pair_ids)
    )
    token_source = sources // 2
    send_rows = jnp.take(tokens, token_source, axis=0, mode="fill", fill_value=0).reshape(
        expert_count, capacity, model_width
    )
    send_grads = jnp.take(out_grad, token_source, axis=0, mode="fill", fill_value=0).reshape(
        expert_count, capacity, model_width
    )
    send_gates = jnp.take(
        gate_values.reshape(-1), sources, axis=0, mode="fill", fill_value=0
    ).reshape(expert_count, capacity)
    full_gate, full_up, full_down = (
        lax.all_gather(gate_weight[0], "dp", axis=0, tiled=True),
        lax.all_gather(up_weight[0], "dp", axis=0, tiled=True),
        lax.all_gather(down_weight[0], "dp", axis=0, tiled=True),
    )

    def duplicate(source_array):
        widened = jnp.broadcast_to(
            source_array[:, None], (source_array.shape[0], seq_count) + source_array.shape[1:]
        )
        return widened.reshape((source_array.shape[0] * seq_count,) + source_array.shape[1:])

    got_rows, got_grads, got_gates = (
        lax.all_to_all(
            duplicate(send_rows), ("expert", "seq"), split_axis=0, concat_axis=0, tiled=True
        ),
        lax.all_to_all(
            duplicate(send_grads), ("expert", "seq"), split_axis=0, concat_axis=0, tiled=True
        ),
        lax.all_to_all(
            duplicate(send_gates).astype(jnp.bfloat16),
            ("expert", "seq"),
            split_axis=0,
            concat_axis=0,
            tiled=True,
        ).astype(jnp.float32),
    )
    routed_all = got_rows.reshape(-1, model_width)
    grads_all = got_grads.reshape(-1, model_width)
    gates_all = got_gates.reshape(-1)
    hidden, scaled, gate_grad, up_grad, back_grad, gate_inner = expert_half(
        routed_all, grads_all, gates_all, full_gate, full_up, full_down
    )
    contract_first = (((0,), (0,)), ((), ()))
    gate_term = lax.dot_general(
        routed_all, gate_grad, contract_first, preferred_element_type=jnp.float32
    )
    up_term = lax.dot_general(
        routed_all, up_grad, contract_first, preferred_element_type=jnp.float32
    )
    down_term = lax.dot_general(scaled, hidden, contract_first, preferred_element_type=jnp.float32)
    summed_grads = lax.psum_scatter(
        jnp.concatenate([gate_term, up_term, down_term], axis=1).astype(jnp.bfloat16),
        "dp",
        scatter_dimension=0,
        tiled=True,
    ).astype(jnp.float32)
    back_parts, inner_parts = (
        lax.all_to_all(
            back_grad.reshape(expert_count * seq_count, capacity, model_width),
            ("expert", "seq"),
            split_axis=0,
            concat_axis=0,
            tiled=True,
        ),
        lax.all_to_all(
            gate_inner.reshape(expert_count * seq_count, capacity).astype(jnp.bfloat16),
            ("expert", "seq"),
            split_axis=0,
            concat_axis=0,
            tiled=True,
        ).astype(jnp.float32),
    )
    back_parts = back_parts.reshape(expert_count, seq_count, capacity, model_width)
    slot_grad = jnp.sum(back_parts.astype(jnp.float32), axis=1).astype(jnp.bfloat16)
    slot_inner = jnp.sum(inner_parts.reshape(expert_count, seq_count, capacity), axis=1)
    picked = slot_grad.reshape(-1, model_width)[slot_index].reshape(tok_count, 2, model_width)
    in_grad = jnp.sum(picked.astype(jnp.float32), axis=1).astype(jnp.bfloat16)
    gate_grads = slot_inner.reshape(-1)[slot_index].reshape(tok_count, 2)
    gate_weight_grad = summed_grads[:, :half_width].astype(jnp.bfloat16)[None]
    up_weight_grad = summed_grads[:, half_width : 2 * half_width].astype(jnp.bfloat16)[None]
    down_weight_grad = summed_grads[:, 2 * half_width :].astype(jnp.bfloat16)[None]
    return (in_grad, gate_grads, gate_weight_grad, up_weight_grad, down_weight_grad)


def solution(mesh):
    return jax.shard_map(
        per_device,
        mesh=mesh,
        in_specs=(
            P(("dp", "expert", "seq"), None),
            P(("dp", "expert", "seq"), None),
            P(("dp", "expert", "seq"), None),
            P(("dp", "expert", "seq"), None),
            P("expert", "dp", "seq"),
            P("expert", "dp", "seq"),
            P("expert", "dp", "seq"),
        ),
        out_specs=(
            P(("dp", "expert", "seq"), None),
            P(("dp", "expert", "seq"), None),
            P("expert", "dp", "seq"),
            P("expert", "dp", "seq"),
            P("expert", "dp", "seq"),
        ),
        check_vma=False,
    )
```

profile of v0, /device:TPU:0, one launch (start us, length us, event | category | flops | bytes accessed | tf_op | source)
XLA Modules:
  0.0 231.6 jit_solution(122135648007683980)
XLA Ops:
  7.2 0.7 broadcast_multiply_fusion
  7.9 0.8 copy.39
  8.7 0.1 eq.29
  8.8 0.1 eq.25
  9.0 0.8 copy.43
  9.8 0.1 reshape.155
  9.9 0.1 copy.38
  10.1 0.1 mul.53
  10.2 1.2 reduce-window.6
  11.4 0.1 slice.33
  11.5 0.1 copy.41
  11.7 0.1 copy.42
  11.8 0.1 add_bitcast_fusion
  11.9 1.4 scatter_custom_fusion
  13.3 2.7 %gather_fusion = bf16[384]{0:T(512)(128)(2,1)S(1)} fusion(bf16[256]{0:T(256)(128)(2,1)S(1)} %reshape.155, s32[1024]{0:T(1024)S(1)} %pad_clamp_fusion.2), kind=kCustom, calls=%fused_computation.2 | custom fusion | bytes 3072 | tf_op jit(solution)/shard_map/jit(_take)/gather | solution.py:59
  16.0 0.1 convert_element_type.89
  16.1 0.6 copy.44
  16.7 5.2 %all-to-all-start = ((bf16[8,1,96]{2,1,0:T(2,128)(2,1)}), bf16[8,1,96]{2,1,0:T(2,128)(2,1)S(1)}, u32[]{:S(2)}, u32[]{:S(2)}) async-start(bf16[8,1,96]{2,1,0:T(2,128)(2,1)} %copy.44), calls=%async_computation | async-start | bytes 8192 | tf_op jit(solution)/shard_map/all_to_all | solution.py:81
  22.0 3.1 %gather_fusion.4 = bf16[384,2048]{1,0:T(8,128)(2,1)} fusion(bf16[128,2048]{1,0:T(8,128)(2,1)S(1)} %copy-done, s32[1024]{0:T(1024)S(1)} %pad_clamp_fusion.1), kind=kCustom, calls=%fused_computation.1.clone | custom fusion | bytes 3147264 | tf_op jit(solution)/shard_map/jit(_take)/gather | solution.py:53
  25.1 3.1 %gather_fusion.3 = bf16[384,2048]{1,0:T(8,128)(2,1)} fusion(bf16[128,2048]{1,0:T(8,128)(2,1)S(1)} %copy-done.1, s32[1024]{0:T(1024)S(1)} %pad_clamp_fusion.1), kind=kCustom, calls=%fused_computation.clone | custom fusion | bytes 3147264 | tf_op jit(solution)/shard_map/jit(_take)/gather | solution.py:56
  28.2 3.3 %broadcast_select_fusion.1 = (bf16[384,2048]{1,0:T(8,128)(2,1)S(1)}, bf16[384,2048]{1,0:T(8,128)(2,1)}) fusion(bf16[384,2048]{1,0:T(8,128)(2,1)} %gather_fusion.3, pred[384]{0:T(512)(128)(4,1)S(1)} %get-tuple-element.26, bf16[384,2048]{1,0:T(8,128)(2,1)} %gather_fusion.4), kind=kLoop, calls=%fused_computation.17 | loop fusion | flops 1572864 | bytes 6291840 | tf_op jit(solution)/shard_map/jit(_take)/select_n | solution.py:56
  31.5 3.5 %broadcast_in_dim.59 = bf16[4,2,96,2048]{3,2,1,0:T(8,128)(2,1)} broadcast(bf16[4,96,2048]{2,1,0:T(8,128)(2,1)} %bitcast.72), dimensions={0,2,3} | broadcast | bytes 4718592 | tf_op jit(solution)/shard_map/broadcast_in_dim | solution.py:69
  35.0 4.4 %all-to-all-start.2 = ((bf16[8,96,2048]{2,1,0:T(8,128)(2,1)}), bf16[8,96,2048]{2,1,0:T(8,128)(2,1)}, u32[]{:S(2)}, u32[]{:S(2)}) async-start(bf16[8,96,2048]{2,1,0:T(8,128)(2,1)} %bitcast.69), calls=%async_computation.2 | async-start | bytes 6291456 | tf_op jit(solution)/shard_map/all_to_all | solution.py:75
  39.5 0.7 all-gather.11.cloned.1.call-update
  40.2 37.1 %all-to-all-done.2 = bf16[8,96,2048]{2,1,0:T(8,128)(2,1)} async-done(((bf16[8,96,2048]{2,1,0:T(8,128)(2,1)}), bf16[8,96,2048]{2,1,0:T(8,128)(2,1)}, u32[]{:S(2)}, u32[]{:S(2)}) %all-to-all-start.2) | async-done | bytes 3145760 | tf_op jit(solution)/shard_map/all_to_all | solution.py:75
  77.3 2.1 broadcast_in_dim.57
  79.4 4.4 %all-to-all-start.1 = ((bf16[8,96,2048]{2,1,0:T(8,128)(2,1)}), bf16[8,96,2048]{2,1,0:T(8,128)(2,1)}, u32[]{:S(2)}, u32[]{:S(2)}) async-start(bf16[8,96,2048]{2,1,0:T(8,128)(2,1)} %bitcast.68), calls=%async_computation.1 | async-start | bytes 6291456 | tf_op jit(solution)/shard_map/all_to_all | solution.py:78
  83.8 0.0 all-gather.7.cloned.1.call-start
  83.9 0.7 all-gather.7.cloned.1.call-update
  84.6 0.7 all-gather.9.cloned.1.call-update
  85.3 0.2 reduce-scatter.2.cloned.1.call-start
  85.6 0.1 reshape.165
  85.7 3.2 %fusion.4 = f32[768,256]{1,0:T(8,128)S(1)} fusion(bf16[768,2048]{1,0:T(8,128)(2,1)} %bitcast.11, bf16[1,2048,256]{2,1,0:T(8,128)(2,1)} %all-gather.11.cloned.1.call-done), kind=kOutput, calls=%fused_computation.20 | convolution fusion | flops 805306368 | bytes 4980736 | tf_op jit(solution)/shard_map/dot_general | solution.py:18
  88.8 32.9 %all-to-all-done.1 = bf16[8,96,2048]{2,1,0:T(8,128)(2,1)} async-done(((bf16[8,96,2048]{2,1,0:T(8,128)(2,1)}), bf16[8,96,2048]{2,1,0:T(8,128)(2,1)}, u32[]{:S(2)}, u32[]{:S(2)}) %all-to-all-start.1) | async-done | bytes 3145760 | tf_op jit(solution)/shard_map/all_to_all | solution.py:78
  121.7 4.2 %fusion = bf16[768,2048]{1,0:T(8,128)(2,1)} fusion(bf16[8,96,2048]{2,1,0:T(8,128)(2,1)} %all-to-all-done.1, f32[768]{0:T(1024)S(1)} %reshape.165), kind=kLoop, calls=%fused_computation.8 | loop fusion | flops 4718592 | bytes 6294528 | tf_op jit(solution)/shard_map/convert_element_type | solution.py:25
  125.9 3.2 %fusion.10 = f32[768,256]{1,0:T(8,128)S(1)} fusion(bf16[768,2048]{1,0:T(8,128)(2,1)} %fusion, bf16[1,2048,256]{2,1,0:T(8,128)(2,1)} %all-gather.7.cloned.1.call-done), kind=kOutput, calls=%fused_computation.26 | convolution fusion | flops 805306368 | bytes 4980736 | tf_op jit(solution)/shard_map/dot_general | solution.py:26
  129.1 15.8 %all-gather.9.cloned.1.call-done = bf16[1,2048,256]{2,1,0:T(8,128)(2,1)} async-done(((bf16[1,512,256]{2,1,0:T(8,128)(2,1)}), bf16[1,2048,256]{2,1,0:T(8,128)(2,1)}) %all-gather.9.cloned.1.call-update) | async-done | bytes 1048592 | tf_op jit(solution)/shard_map/all_gather | solution.py:64
  144.8 3.5 %multiply_convert_fusion = (bf16[768,256]{1,0:T(8,128)(2,1)S(1)}, bf16[768,256]{1,0:T(8,128)(2,1)S(1)}, bf16[768,256]{1,0:T(8,128)(2,1)S(1)}) fusion(f32[768,256]{1,0:T(8,128)S(1)} %fusion.4, f32[768,256]{1,0:T(8,128)S(1)} %fusion.10, bf16[768,2048]{1,0:T(8,128)(2,1)} %bitcast.11, bf16[1,2048,256]{2,1,0:T(8,128)(2,1)} %all-gather.9.cloned.1.call-done), kind=kOutput, calls=%fused_computation.28 | convolution fusion | flops 808255488 | bytes 6946816 | tf_op jit(solution)/shard_map/dot_general | solution.py:19
  148.4 1.0 convolution_convert_fusion
  149.5 2.9 %convolution_convert_fusion.2 = bf16[2048,256]{0,1:T(8,128)(2,1)S(1)} fusion(bf16[768,2048]{1,0:T(8,128)(2,1)} %bitcast.11, bf16[768,256]{1,0:T(8,128)(2,1)S(1)} %get-tuple-element.29), kind=kOutput, calls=%fused_computation.15 | convolution fusion | flops 805830656 | bytes 4587520 | tf_op jit(solution)/shard_map/dot_general | solution.py:96
  152.4 2.9 %convolution_convert_fusion.1 = bf16[2048,256]{0,1:T(8,128)(2,1)S(1)} fusion(bf16[768,2048]{1,0:T(8,128)(2,1)} %bitcast.11, bf16[768,256]{1,0:T(8,128)(2,1)S(1)} %get-tuple-element.30), kind=kOutput, calls=%fused_computation.14 | convolution fusion | flops 805830656 | bytes 4587520 | tf_op jit(solution)/shard_map/dot_general | solution.py:99
  155.3 1.9 pad_maximum_fusion
  157.2 1.2 copy-done.5
  158.4 3.2 %fusion.1 = bf16[768]{0:T(1024)(128)(2,1)S(1)} fusion(bf16[768,2048]{1,0:T(8,128)(2,1)} %bitcast.17, bf16[768,256]{1,0:T(8,128)(2,1)} %copy-done.6, bf16[1,2048,256]{2,1,0:T(8,128)(2,1)S(1)} %copy-done.5), kind=kOutput, calls=%fused_computation.9 | convolution fusion | flops 810024192 | bytes 4589056 | tf_op jit(solution)/shard_map/dot_general | solution.py:23
  161.6 0.7 convert_element_type.107
  162.3 3.7 %all-to-all-start.4 = ((bf16[8,1,96]{2,1,0:T(2,128)(2,1)}), bf16[8,1,96]{2,1,0:T(2,128)(2,1)S(1)}, u32[]{:S(2)}, u32[]{:S(2)}) async-start(bf16[8,1,96]{2,1,0:T(2,128)(2,1)} %convert_element_type.107), calls=%async_computation.4 | async-start | bytes 8192 | tf_op jit(solution)/shard_map/all_to_all | solution.py:117
  166.0 1.0 fusion.2
  167.0 0.2 copy-done.4
  167.2 2.8 %add_convert_fusion = bf16[768,2048]{1,0:T(8,128)(2,1)} fusion(f32[768,2048]{1,0:T(8,128)S(1)} %fusion.2, bf16[768,256]{1,0:T(8,128)(2,1)S(1)} %get-tuple-element.30, bf16[1,2048,256]{2,1,0:T(8,128)(2,1)S(1)} %copy-done.4), kind=kOutput, calls=%fused_computation.10 | convolution fusion | flops 808452096 | bytes 10878976 | tf_op jit(solution)/shard_map/dot_general | solution.py:34
  170.0 0.6 all-to-all-done.4
  170.6 4.7 %all-to-all-start.3 = ((bf16[8,96,2048]{2,1,0:T(8,128)(2,1)}), bf16[8,96,2048]{2,1,0:T(8,128)(2,1)}, u32[]{:S(2)}, u32[]{:S(2)}) async-start(bf16[8,96,2048]{2,1,0:T(8,128)(2,1)} %bitcast.70), calls=%async_computation.3 | async-start | bytes 6291456 | tf_op jit(solution)/shard_map/all_to_all | solution.py:110
  175.3 0.1 reshape.163
  175.4 1.9 gather_fusion.2
  177.3 0.1 reshape.164
  177.5 0.6 copy.46
  178.1 34.8 %all-to-all-done.3 = bf16[8,96,2048]{2,1,0:T(8,128)(2,1)} async-done(((bf16[8,96,2048]{2,1,0:T(8,128)(2,1)}), bf16[8,96,2048]{2,1,0:T(8,128)(2,1)}, u32[]{:S(2)}, u32[]{:S(2)}) %all-to-all-start.3) | async-done | bytes 3145760 | tf_op jit(solution)/shard_map/all_to_all | solution.py:110
  212.9 2.8 %bitcast_reduce_fusion = bf16[4,96,2048]{2,1,0:T(8,128)(2,1)S(1)} fusion(bf16[8,96,2048]{2,1,0:T(8,128)(2,1)} %all-to-all-done.3), kind=kLoop, calls=%fused_computation.12 | loop fusion | flops 786432 | bytes 4718592 | tf_op jit(solution)/shard_map/reduce_sum | solution.py:126
  215.6 1.4 gather_fusion.1
  217.0 0.7 reshape.162
  217.7 3.6 %reduce_sum.56 = bf16[128,2048]{1,0:T(8,128)(2,1)} reduce(bf16[128,2,2048]{2,1,0:T(2,128)(2,1)S(1)} %reshape.162, bf16[]{:T(256)} %constant.57.clone.1), dimensions={1}, to_apply=%region_5.7 | reduce | flops 262144 | bytes 1572866 | tf_op jit(solution)/shard_map/reduce_sum | solution.py:129
  221.4 1.2 slice_bitcast_fusion
  222.5 0.8 copy.49
  223.4 0.8 copy.48
  224.2 0.8 copy.47
  (35 shorter events, 0.3 us)
Async XLA Ops:
  7.2 14.8 %copy-start = (bf16[128,2048]{1,0:T(8,128)(2,1)S(1)}, bf16[128,2048]{1,0:T(8,128)(2,1)}, u32[]{:S(2)}) copy-start(bf16[128,2048]{1,0:T(8,128)(2,1)} %param.9) | copy-start | bytes 1572868
  16.7 14.8 %all-to-all-start = ((bf16[8,1,96]{2,1,0:T(2,128)(2,1)}), bf16[8,1,96]{2,1,0:T(2,128)(2,1)S(1)}, u32[]{:S(2)}, u32[]{:S(2)}) async-start(bf16[8,1,96]{2,1,0:T(2,128)(2,1)} %copy.44), calls=%async_computation | async-start | bytes 8192 | tf_op jit(solution)/shard_map/all_to_all | solution.py:81
  22.0 3.1 %copy-start.1 = (bf16[128,2048]{1,0:T(8,128)(2,1)S(1)}, bf16[128,2048]{1,0:T(8,128)(2,1)}, u32[]{:S(2)}) copy-start(bf16[128,2048]{1,0:T(8,128)(2,1)} %param.10) | copy-start | bytes 1572868
  35.0 42.3 %all-to-all-start.2 = ((bf16[8,96,2048]{2,1,0:T(8,128)(2,1)}), bf16[8,96,2048]{2,1,0:T(8,128)(2,1)}, u32[]{:S(2)}, u32[]{:S(2)}) async-start(bf16[8,96,2048]{2,1,0:T(8,128)(2,1)} %bitcast.69), calls=%async_computation.2 | async-start | bytes 6291456 | tf_op jit(solution)/shard_map/all_to_all | solution.py:75
  39.4 46.2 %all-gather.11.cloned.1.call-start = ((), (), s32[]{:S(2)}) async-start(), calls=%async_computation.9 | async-start | bytes 1310720 | tf_op jit(solution)/shard_map/all_gather | solution.py:63
  79.4 42.3 %all-to-all-start.1 = ((bf16[8,96,2048]{2,1,0:T(8,128)(2,1)}), bf16[8,96,2048]{2,1,0:T(8,128)(2,1)}, u32[]{:S(2)}, u32[]{:S(2)}) async-start(bf16[8,96,2048]{2,1,0:T(8,128)(2,1)} %bitcast.68), calls=%async_computation.1 | async-start | bytes 6291456 | tf_op jit(solution)/shard_map/all_to_all | solution.py:78
  83.8 42.1 %all-gather.7.cloned.1.call-start = ((), (), s32[]{:S(2)}) async-start(), calls=%async_computation.7 | async-start | bytes 1310720 | tf_op jit(solution)/shard_map/all_gather | solution.py:65
  84.6 60.2 %all-gather.9.cloned.1.call-start = ((), (), s32[]{:S(2)}) async-start(), calls=%async_computation.8 | async-start | bytes 1310720 | tf_op jit(solution)/shard_map/all_gather | solution.py:64
  85.3 136.0 %reduce-scatter.2.cloned.1.call-start = ((), (), s32[]{:S(2)}) async-start(), calls=%async_computation.6 | async-start | bytes 3932160 | tf_op jit(solution)/shard_map/reduce_scatter | solution.py:103
  144.8 3.6 %copy-start.2 = (bf16[768,2048]{1,0:T(8,128)(2,1)S(1)}, bf16[768,2048]{1,0:T(8,128)(2,1)}, u32[]{:S(2)}) copy-start(bf16[768,2048]{1,0:T(8,128)(2,1)} %fusion) | copy-start | bytes 9437188
  148.4 1.1 copy-start.6
  157.2 1.2 copy-start.5
  158.4 7.6 %copy-start.3 = (bf16[1,2048,256]{2,1,0:T(8,128)(2,1)S(1)}, bf16[1,2048,256]{2,1,0:T(8,128)(2,1)}, u32[]{:S(2)}) copy-start(bf16[1,2048,256]{2,1,0:T(8,128)(2,1)} %all-gather.11.cloned.1.call-done) | copy-start | bytes 3145732
  162.3 8.3 %all-to-all-start.4 = ((bf16[8,1,96]{2,1,0:T(2,128)(2,1)}), bf16[8,1,96]{2,1,0:T(2,128)(2,1)S(1)}, u32[]{:S(2)}, u32[]{:S(2)}) async-start(bf16[8,1,96]{2,1,0:T(2,128)(2,1)} %convert_element_type.107), calls=%async_computation.4 | async-start | bytes 8192 | tf_op jit(solution)/shard_map/all_to_all | solution.py:117
  166.0 1.2 copy-start.4
  170.6 42.3 %all-to-all-start.3 = ((bf16[8,96,2048]{2,1,0:T(8,128)(2,1)}), bf16[8,96,2048]{2,1,0:T(8,128)(2,1)}, u32[]{:S(2)}, u32[]{:S(2)}) async-start(bf16[8,96,2048]{2,1,0:T(8,128)(2,1)} %bitcast.70), calls=%async_computation.3 | async-start | bytes 6291456 | tf_op jit(solution)/shard_map/all_to_all | solution.py:110
Sparse Core Ops, SparseCore 0:
  41.8 29.6 all-gather.10
  86.2 29.5 all-gather.6
  117.4 27.3 all-gather.8
  157.3 59.8 reduce-scatter.1
where the time goes:
time: 232 us
  waiting for transfers between devices  123 us (53%)
  local copies, waits for them, and re-layouts  29.9 us (13%)
  matrix products  23.7 us (10%)
  starting transfers between devices  22.8 us (10%)
  other arithmetic  18 us (8%)
  between operations  14 us (6%)
    all_to_all x1, waiting for transfers between devices, per_device(): lax.all_to_all(duplicate(send_rows), ('expert', 'seq'), split_axis=0, con...  37.1 us
    all_to_all x1, waiting for transfers between devices, per_device(): lax.all_to_all(back_grad.reshape(expert_count * seq_count, capacity, mode...  34.8 us
    all_to_all x1, waiting for transfers between devices, per_device(): lax.all_to_all(duplicate(send_grads), ('expert', 'seq'), split_axis=0, co...  32.9 us
    all_gather x1, waiting for transfers between devices, per_device(): lax.all_gather(up_weight[0], 'dp', axis=0, tiled=True)  15.8 us
    unnamed x20, local copies, waits for them, and re-layouts  6.18 us
    broadcast_in_dim x3, local copies, waits for them, and re-layouts, duplicate(): jnp.broadcast_to(source_array[:, None], (source_array.shape[0], seq_count...  5.55 us
    all_to_all x1, starting transfers between devices, per_device(): lax.all_to_all(duplicate(send_gates).astype(jnp.bfloat16), ('expert', 'se...  5.2 us
    all_to_all x1, starting transfers between devices, per_device(): lax.all_to_all(back_grad.reshape(expert_count * seq_count, capacity, mode...  4.67 us
  transfers between devices with their start and end apart: 9, of which 5 were waited for; matrix products, arithmetic and copies ran while one was open for 18% of the time, Pallas kernels for 0%

commit v1 on v0

--- a/solution.py
+++ b/solution.py
@@ -2,6 +2,22 @@
 import jax.numpy as jnp
 from jax import lax
 from jax.sharding import PartitionSpec as P
+
+
+def pairwise_exchange(value, axis, split, join):
+    ways, here = (lax.axis_size(axis), lax.axis_index(axis))
+    width = value.shape[split] // ways
+    shape = list(value.shape)
+    shape[split] = width
+    height = shape[join]
+    shape[join] = height * ways
+    full = jnp.zeros(shape, value.dtype)
+    for mask in range(ways):
+        part = lax.dynamic_slice_in_dim(value, (here ^ mask) * width, width, axis=split)
+        if mask:
+            part = lax.ppermute(part, axis, [(d, d ^ mask) for d in range(ways)])
+        full = lax.dynamic_update_slice_in_dim(full, part, (here ^ mask) * height, axis=join)
+    return full
 
 
 def route_slots(block_ids, expert_count, capacity):
@@ -75,9 +91,7 @@
         lax.all_to_all(
             duplicate(send_rows), ("expert", "seq"), split_axis=0, concat_axis=0, tiled=True
         ),
-        lax.all_to_all(
-            duplicate(send_grads), ("expert", "seq"), split_axis=0, concat_axis=0, tiled=True
-        ),
+        pairwise_exchange(duplicate(send_grads), ("expert", "seq"), 0, 0),
         lax.all_to_all(
             duplicate(send_gates).astype(jnp.bfloat16),
             ("expert", "seq"),

time: 232 us -> 210 us (0.905)
  waiting for transfers between devices: 123 us -> 92 us
  local copies, waits for them, and re-layouts: 29.9 us -> 37 us
    ppermute x0 -> x7, waiting for transfers between devices: none -> 55.2 us  [pairwise_exchange(): part = lax.ppermute(part, axis, [(d, d ^ mask) for d in range(ways)])]
    all_to_all x1, waiting for transfers between devices: 37.1 us -> 0.01 us  [per_device(): lax.all_to_all(duplicate(send_rows), ('expert', 'seq'), split_axis=0, con...]
    all_to_all x1 -> x0, waiting for transfers between devices: 32.9 us -> none  [per_device(): lax.all_to_all(duplicate(send_grads), ('expert', 'seq'), split_axis=0, co...]
    all_gather x1, waiting for transfers between devices: 15.8 us -> 0.02 us  [per_device(): lax.all_gather(up_weight[0], 'dp', axis=0, tiled=True)]
    ppermute x0 -> x7, starting transfers between devices: none -> 6.65 us  [pairwise_exchange(): part = lax.ppermute(part, axis, [(d, d ^ mask) for d in range(ways)])]
    dynamic_update_slice x0 -> x7, local copies, waits for them, and re-layouts: none -> 5.61 us  [pairwise_exchange(): lax.dynamic_update_slice_in_dim(full, part, (here ^ mask) * height, axis=...]
    all_to_all x1 -> x0, starting transfers between devices: 4.44 us -> none  [per_device(): lax.all_to_all(duplicate(send_grads), ('expert', 'seq'), split_axis=0, co...]
    unnamed x20 -> x22, local copies, waits for them, and re-layouts: 6.18 us -> 7.66 us
  transfers between devices with their start and end apart: 9 -> 15, of which waited for: 5 -> 6; matrix products, arithmetic and copies ran while one was open for 18% -> 29% of each run, Pallas kernels for 0% -> 0%
where the time goes in v1:
time: 210 us; the launch traced here: 209 us
  waiting for transfers between devices  92 us (44%)
  local copies, waits for them, and re-layouts  37 us (18%)
  starting transfers between devices  24.6 us (12%)
  matrix products  23.9 us (11%)
  other arithmetic  17.8 us (8%)
  between operations  14.1 us (7%)
    ppermute x7, waiting for transfers between devices, pairwise_exchange(): part = lax.ppermute(part, axis, [(d, d ^ mask) for d in range(ways)])  55.2 us
    all_to_all x1, waiting for transfers between devices, per_device(): lax.all_to_all(back_grad.reshape(expert_count * seq_count, capacity, mode...  34.8 us
    unnamed x22, local copies, waits for them, and re-layouts  7.66 us
    ppermute x7, starting transfers between devices, pairwise_exchange(): part = lax.ppermute(part, axis, [(d, d ^ mask) for d in range(ways)])  6.65 us
    dynamic_update_slice x7, local copies, waits for them, and re-layouts, pairwise_exchange(): lax.dynamic_update_slice_in_dim(full, part, (here ^ mask) * height, axis=...  5.61 us
    all_to_all x1, starting transfers between devices, per_device(): lax.all_to_all(duplicate(send_gates).astype(jnp.bfloat16), ('expert', 'se...  5.2 us
    all_to_all x1, starting transfers between devices, per_device(): lax.all_to_all(back_grad.reshape(expert_count * seq_count, capacity, mode...  4.67 us
    all_to_all x1, starting transfers between devices, per_device(): lax.all_to_all(duplicate(send_rows), ('expert', 'seq'), split_axis=0, con...  4.44 us
  transfers between devices with their start and end apart: 15, of which 6 were waited for; matrix products, arithmetic and copies ran while one was open for 29% of the time, Pallas kernels for 0%

profile of v1, /device:TPU:0, one launch (start us, length us, event | category | flops | bytes accessed | tf_op | source)
XLA Modules:
  0.0 209.4 jit_solution(2579090520039520201)
XLA Ops:
  7.2 0.7 all-gather.11.cloned.1.call-update
  8.0 0.7 all-gather.9.cloned.1.call-update
  8.7 0.8 copy.39
  9.7 0.7 broadcast_multiply_fusion
  10.4 1.2 reduce-window.6
  12.3 1.4 scatter_custom_fusion
  13.8 0.8 copy.43
  14.7 2.7 %gather_fusion = bf16[384]{0:T(512)(128)(2,1)S(1)} fusion(bf16[256]{0:T(256)(128)(2,1)S(1)} %reshape.155, s32[1024]{0:T(1024)S(1)} %pad_clamp_fusion.2), kind=kCustom, calls=%fused_computation.2 | custom fusion | bytes 3072 | tf_op jit(solution)/shard_map/jit(_take)/gather | solution.py:75
  17.5 0.6 copy.44
  18.1 5.2 %all-to-all-start = ((bf16[8,1,96]{2,1,0:T(2,128)(2,1)}), bf16[8,1,96]{2,1,0:T(2,128)(2,1)S(1)}, u32[]{:S(2)}, u32[]{:S(2)}) async-start(bf16[8,1,96]{2,1,0:T(2,128)(2,1)} %copy.44), calls=%async_computation | async-start | bytes 8192 | tf_op jit(solution)/shard_map/all_to_all | solution.py:95
  23.4 3.1 %gather_fusion.3 = bf16[384,2048]{1,0:T(8,128)(2,1)} fusion(bf16[128,2048]{1,0:T(8,128)(2,1)S(1)} %copy-done, s32[1024]{0:T(1024)S(1)} %pad_clamp_fusion.1), kind=kCustom, calls=%fused_computation.clone | custom fusion | bytes 3147264 | tf_op jit(solution)/shard_map/jit(_take)/gather | solution.py:72
  26.5 3.1 %gather_fusion.4 = bf16[384,2048]{1,0:T(8,128)(2,1)} fusion(bf16[128,2048]{1,0:T(8,128)(2,1)S(1)} %copy-done.1, s32[1024]{0:T(1024)S(1)} %pad_clamp_fusion.1), kind=kCustom, calls=%fused_computation.1.clone | custom fusion | bytes 3147264 | tf_op jit(solution)/shard_map/jit(_take)/gather | solution.py:69
  29.6 3.3 %broadcast_select_fusion.1 = (bf16[384,2048]{1,0:T(8,128)(2,1)S(1)}, bf16[384,2048]{1,0:T(8,128)(2,1)}) fusion(bf16[384,2048]{1,0:T(8,128)(2,1)} %gather_fusion.3, pred[384]{0:T(512)(128)(4,1)S(1)} %get-tuple-element.26, bf16[384,2048]{1,0:T(8,128)(2,1)} %gather_fusion.4), kind=kLoop, calls=%fused_computation.17 | loop fusion | flops 1572864 | bytes 6291840 | tf_op jit(solution)/shard_map/jit(_take)/select_n | solution.py:72
  33.0 3.5 %broadcast_in_dim.63 = bf16[4,2,96,2048]{3,2,1,0:T(8,128)(2,1)} broadcast(bf16[4,96,2048]{2,1,0:T(8,128)(2,1)} %bitcast.72), dimensions={0,2,3} | broadcast | bytes 4718592 | tf_op jit(solution)/shard_map/broadcast_in_dim | solution.py:85
  36.5 4.4 %all-to-all-start.1 = ((bf16[8,96,2048]{2,1,0:T(8,128)(2,1)}), bf16[8,96,2048]{2,1,0:T(8,128)(2,1)}, u32[]{:S(2)}, u32[]{:S(2)}) async-start(bf16[8,96,2048]{2,1,0:T(8,128)(2,1)} %bitcast.67), calls=%async_computation.1 | async-start | bytes 6291456 | tf_op jit(solution)/shard_map/all_to_all | solution.py:91
  41.0 0.4 broadcast_in_dim.61
  41.3 0.4 broadcast_in_dim.59
  41.7 1.3 constant_dynamic-slice_fusion
  43.1 1.7 copy-done.2
  44.8 0.4 collective-permute-start
  45.2 1.6 collective-permute-start.1
  46.9 1.7 collective-permute-start.3
  48.7 0.2 reduce-scatter.2.cloned.1.call-start
  49.1 2.6 %collective-permute-start.5 = (bf16[1,96,2048]{2,1,0:T(8,128)(2,1)S(1)}, bf16[1,96,2048]{2,1,0:T(8,128)(2,1)S(1)}, u32[]{:S(2)}, u32[]{:S(2)}) collective-permute-start(bf16[1,96,2048]{2,1,0:T(8,128)(2,1)S(1)} %get-tuple-element.29), channel_id=1, source_target_pairs={{0,6},{1,7},{2,4},{3,5},{4,2},{5,3},{6,0},{7,1},{8,14},{9,15},{10,... | collective-permute-start | bytes 1179656 | tf_op jit(solution)/shard_map/ppermute | solution.py:18
  51.6 0.8 constant_dynamic-update-slice_fusion.5
  52.4 34.4 %collective-permute-done.1 = bf16[1,96,2048]{2,1,0:T(8,128)(2,1)S(1)} collective-permute-done((bf16[1,96,2048]{2,1,0:T(8,128)(2,1)}, bf16[1,96,2048]{2,1,0:T(8,128)(2,1)S(1)}, u32[]{:S(2)}, u32[]{:S(2)}) %collective-permute-start.1) | collective-permute-done | bytes 393248 | tf_op jit(solution)/shard_map/ppermute | solution.py:18
  86.8 0.2 collective-permute-start.6
  86.9 0.8 constant_dynamic-update-slice_fusion.4
  87.7 6.4 %collective-permute-done.2 = bf16[1,96,2048]{2,1,0:T(8,128)(2,1)S(1)} collective-permute-done((bf16[1,96,2048]{2,1,0:T(8,128)(2,1)}, bf16[1,96,2048]{2,1,0:T(8,128)(2,1)S(1)}, u32[]{:S(2)}, u32[]{:S(2)}) %collective-permute-start.2) | collective-permute-done | bytes 393248 | tf_op jit(solution)/shard_map/ppermute | solution.py:18
  94.1 0.8 constant_dynamic-update-slice_fusion.3
  94.9 0.8 constant_dynamic-update-slice_fusion.2
  95.7 0.8 constant_dynamic-update-slice_fusion.1
  96.5 8.0 %collective-permute-done.5 = bf16[1,96,2048]{2,1,0:T(8,128)(2,1)S(1)} collective-permute-done((bf16[1,96,2048]{2,1,0:T(8,128)(2,1)S(1)}, bf16[1,96,2048]{2,1,0:T(8,128)(2,1)S(1)}, u32[]{:S(2)}, u32[]{:S(2)}) %collective-permute-start.5) | collective-permute-done | bytes 393248 | tf_op jit(solution)/shard_map/ppermute | solution.py:18
  104.6 0.8 constant_dynamic-update-slice_fusion
  105.4 6.5 %collective-permute-done.6 = bf16[1,96,2048]{2,1,0:T(8,128)(2,1)S(1)} collective-permute-done((bf16[1,96,2048]{2,1,0:T(8,128)(2,1)S(1)}, bf16[1,96,2048]{2,1,0:T(8,128)(2,1)S(1)}, u32[]{:S(2)}, u32[]{:S(2)}) %collective-permute-start.6) | collective-permute-done | bytes 393248 | tf_op jit(solution)/shard_map/ppermute | solution.py:18
  111.8 0.8 constant_dynamic-update-slice_fusion.6
  112.7 4.1 %fusion = bf16[768,2048]{1,0:T(8,128)(2,1)} fusion(bf16[8,96,2048]{2,1,0:T(8,128)(2,1)} %constant_dynamic-update-slice_fusion.6, f32[768]{0:T(1024)S(1)} %reshape.165), kind=kLoop, calls=%fused_computation.8 | loop fusion | flops 4718592 | bytes 6294528 | tf_op jit(solution)/shard_map/convert_element_type | solution.py:41
  116.8 3.2 %fusion.4 = f32[768,256]{1,0:T(8,128)S(1)} fusion(bf16[768,2048]{1,0:T(8,128)(2,1)} %bitcast.11, bf16[1,2048,256]{2,1,0:T(8,128)(2,1)} %all-gather.11.cloned.1.call-done), kind=kOutput, calls=%fused_computation.20 | convolution fusion | flops 805306368 | bytes 4980736 | tf_op jit(solution)/shard_map/dot_general | solution.py:34
  120.0 3.2 %fusion.7 = f32[768,256]{1,0:T(8,128)S(1)} fusion(bf16[768,2048]{1,0:T(8,128)(2,1)} %bitcast.11, bf16[1,2048,256]{2,1,0:T(8,128)(2,1)} %all-gather.9.cloned.1.call-done), kind=kOutput, calls=%fused_computation.23 | convolution fusion | flops 805306368 | bytes 4980736 | tf_op jit(solution)/shard_map/dot_general | solution.py:35
  123.2 3.5 %multiply_convert_fusion = (bf16[768,256]{1,0:T(8,128)(2,1)S(1)}, bf16[768,256]{1,0:T(8,128)(2,1)S(1)}, bf16[768,256]{1,0:T(8,128)(2,1)S(1)}) fusion(f32[768,256]{1,0:T(8,128)S(1)} %fusion.7, f32[768,256]{1,0:T(8,128)S(1)} %fusion.4, bf16[768,2048]{1,0:T(8,128)(2,1)} %fusion, bf16[1,2048,256]{2,1,0:T(8,128)(2,1)} %all-gather.7.cloned.1.call-done), kind=kOutput, calls=%fused_computation.28 | convolution fusion | flops 808255488 | bytes 6946816 | tf_op jit(solution)/shard_map/dot_general | solution.py:42
  126.7 1.0 convolution_convert_fusion
  127.8 2.9 %convolution_convert_fusion.1 = bf16[2048,256]{0,1:T(8,128)(2,1)S(1)} fusion(bf16[768,2048]{1,0:T(8,128)(2,1)} %bitcast.11, bf16[768,256]{1,0:T(8,128)(2,1)S(1)} %get-tuple-element.38), kind=kOutput, calls=%fused_computation.14 | convolution fusion | flops 805830656 | bytes 4587520 | tf_op jit(solution)/shard_map/dot_general | solution.py:113
  130.7 2.9 %convolution_convert_fusion.2 = bf16[2048,256]{0,1:T(8,128)(2,1)S(1)} fusion(bf16[768,2048]{1,0:T(8,128)(2,1)} %bitcast.11, bf16[768,256]{1,0:T(8,128)(2,1)S(1)} %get-tuple-element.37), kind=kOutput, calls=%fused_computation.15 | convolution fusion | flops 805830656 | bytes 4587520 | tf_op jit(solution)/shard_map/dot_general | solution.py:110
  133.6 1.8 pad_maximum_fusion
  135.4 1.0 copy-done.7
  136.4 3.4 %fusion.1 = bf16[768]{0:T(1024)(128)(2,1)S(1)} fusion(bf16[768,2048]{1,0:T(8,128)(2,1)} %bitcast.70, bf16[768,256]{1,0:T(8,128)(2,1)S(1)} %copy-done.7, bf16[1,2048,256]{2,1,0:T(8,128)(2,1)} %all-gather.7.cloned.1.call-done), kind=kOutput, calls=%fused_computation.9 | convolution fusion | flops 810024192 | bytes 4589056 | tf_op jit(solution)/shard_map/dot_general | solution.py:39
  139.8 0.7 convert_element_type.107
  140.5 3.3 %all-to-all-start.3 = ((bf16[8,1,96]{2,1,0:T(2,128)(2,1)}), bf16[8,1,96]{2,1,0:T(2,128)(2,1)S(1)}, u32[]{:S(2)}, u32[]{:S(2)}) async-start(bf16[8,1,96]{2,1,0:T(2,128)(2,1)} %convert_element_type.107), calls=%async_computation.3 | async-start | bytes 8192 | tf_op jit(solution)/shard_map/all_to_all | solution.py:131
  143.8 1.0 fusion.2
  144.8 0.2 copy-done.5
  145.0 2.8 %add_convert_fusion = bf16[768,2048]{1,0:T(8,128)(2,1)} fusion(f32[768,2048]{1,0:T(8,128)S(1)} %fusion.2, bf16[768,256]{1,0:T(8,128)(2,1)S(1)} %get-tuple-element.38, bf16[1,2048,256]{2,1,0:T(8,128)(2,1)S(1)} %copy-done.5), kind=kOutput, calls=%fused_computation.10 | convolution fusion | flops 808452096 | bytes 10878976 | tf_op jit(solution)/shard_map/dot_general | solution.py:50
  147.8 0.5 all-to-all-done.3
  148.3 4.7 %all-to-all-start.2 = ((bf16[8,96,2048]{2,1,0:T(8,128)(2,1)}), bf16[8,96,2048]{2,1,0:T(8,128)(2,1)}, u32[]{:S(2)}, u32[]{:S(2)}) async-start(bf16[8,96,2048]{2,1,0:T(8,128)(2,1)} %bitcast.68), calls=%async_computation.2 | async-start | bytes 6291456 | tf_op jit(solution)/shard_map/all_to_all | solution.py:124
  153.2 1.9 gather_fusion.2
  155.3 0.6 copy.46
  155.9 34.8 %all-to-all-done.2 = bf16[8,96,2048]{2,1,0:T(8,128)(2,1)} async-done(((bf16[8,96,2048]{2,1,0:T(8,128)(2,1)}), bf16[8,96,2048]{2,1,0:T(8,128)(2,1)}, u32[]{:S(2)}, u32[]{:S(2)}) %all-to-all-start.2) | async-done | bytes 3145760 | tf_op jit(solution)/shard_map/all_to_all | solution.py:124
  190.7 2.8 %bitcast_reduce_fusion = bf16[4,96,2048]{2,1,0:T(8,128)(2,1)S(1)} fusion(bf16[8,96,2048]{2,1,0:T(8,128)(2,1)} %all-to-all-done.2), kind=kLoop, calls=%fused_computation.12 | loop fusion | flops 786432 | bytes 4718592 | tf_op jit(solution)/shard_map/reduce_sum | solution.py:140
  193.5 1.4 gather_fusion.1
  194.8 0.7 reshape.162
  195.6 3.6 %reduce_sum.56 = bf16[128,2048]{1,0:T(8,128)(2,1)} reduce(bf16[128,2,2048]{2,1,0:T(2,128)(2,1)S(1)} %reshape.162, bf16[]{:T(256)} %constant.43.clone.1), dimensions={1}, to_apply=%region_5.7 | reduce | flops 262144 | bytes 1572866 | tf_op jit(solution)/shard_map/reduce_sum | solution.py:143
  199.2 1.2 slice_bitcast_fusion
  200.4 0.8 copy.47
  201.2 0.8 copy.48
  202.0 0.8 copy.49
  (58 shorter events, 1.9 us)
Async XLA Ops:
  7.2 16.2 %copy-start = (bf16[128,2048]{1,0:T(8,128)(2,1)S(1)}, bf16[128,2048]{1,0:T(8,128)(2,1)}, u32[]{:S(2)}) copy-start(bf16[128,2048]{1,0:T(8,128)(2,1)} %param.10) | copy-start | bytes 1572868
  7.2 109.6 %all-gather.11.cloned.1.call-start = ((), (), s32[]{:S(2)}) async-start(), calls=%async_computation.8 | async-start | bytes 1310720 | tf_op jit(solution)/shard_map/all_gather | solution.py:79
  7.9 112.0 %all-gather.9.cloned.1.call-start = ((), (), s32[]{:S(2)}) async-start(), calls=%async_computation.7 | async-start | bytes 1310720 | tf_op jit(solution)/shard_map/all_gather | solution.py:80
  18.1 14.8 %all-to-all-start = ((bf16[8,1,96]{2,1,0:T(2,128)(2,1)}), bf16[8,1,96]{2,1,0:T(2,128)(2,1)S(1)}, u32[]{:S(2)}, u32[]{:S(2)}) async-start(bf16[8,1,96]{2,1,0:T(2,128)(2,1)} %copy.44), calls=%async_computation | async-start | bytes 8192 | tf_op jit(solution)/shard_map/all_to_all | solution.py:95
  23.4 3.1 %copy-start.1 = (bf16[128,2048]{1,0:T(8,128)(2,1)S(1)}, bf16[128,2048]{1,0:T(8,128)(2,1)}, u32[]{:S(2)}) copy-start(bf16[128,2048]{1,0:T(8,128)(2,1)} %param.9) | copy-start | bytes 1572868
  36.5 80.3 %all-to-all-start.1 = ((bf16[8,96,2048]{2,1,0:T(8,128)(2,1)}), bf16[8,96,2048]{2,1,0:T(8,128)(2,1)}, u32[]{:S(2)}, u32[]{:S(2)}) async-start(bf16[8,96,2048]{2,1,0:T(8,128)(2,1)} %bitcast.67), calls=%async_computation.1 | async-start | bytes 6291456 | tf_op jit(solution)/shard_map/all_to_all | solution.py:91
  40.9 82.2 %all-gather.7.cloned.1.call-start = ((), (), s32[]{:S(2)}) async-start(), calls=%async_computation.6 | async-start | bytes 1310720 | tf_op jit(solution)/shard_map/all_gather | solution.py:81
  43.1 1.7 copy-start.2
  44.8 4.3 %collective-permute-start = (bf16[1,96,2048]{2,1,0:T(8,128)(2,1)}, bf16[1,96,2048]{2,1,0:T(8,128)(2,1)S(1)}, u32[]{:S(2)}, u32[]{:S(2)}) collective-permute-start(bf16[1,96,2048]{2,1,0:T(8,128)(2,1)} %get-tuple-element.34), channel_id=1, source_target_pairs={{0,1},{1,0},{2,3},{3,2},{4,5},{5,4},{6,7},{7,6},{8,9},{9,8},{10,11... | collective-permute-start | bytes 1179656 | tf_op jit(solution)/shard_map/ppermute | solution.py:18
  45.2 41.5 %collective-permute-start.1 = (bf16[1,96,2048]{2,1,0:T(8,128)(2,1)}, bf16[1,96,2048]{2,1,0:T(8,128)(2,1)S(1)}, u32[]{:S(2)}, u32[]{:S(2)}) collective-permute-start(bf16[1,96,2048]{2,1,0:T(8,128)(2,1)} %get-tuple-element.33), channel_id=1, source_target_pairs={{0,2},{1,3},{2,0},{3,1},{4,6},{5,7},{6,4},{7,5},{8,10},{9,11},{10,... | collective-permute-start | bytes 1179656 | tf_op jit(solution)/shard_map/ppermute | solution.py:18
  46.9 47.2 %collective-permute-start.2 = (bf16[1,96,2048]{2,1,0:T(8,128)(2,1)}, bf16[1,96,2048]{2,1,0:T(8,128)(2,1)S(1)}, u32[]{:S(2)}, u32[]{:S(2)}) collective-permute-start(bf16[1,96,2048]{2,1,0:T(8,128)(2,1)} %get-tuple-element.32), channel_id=1, source_target_pairs={{0,3},{1,2},{2,1},{3,0},{4,7},{5,6},{6,5},{7,4},{8,11},{9,10},{10,... | collective-permute-start | bytes 1179656 | tf_op jit(solution)/shard_map/ppermute | solution.py:18
  46.9 48.0 %collective-permute-start.3 = (bf16[1,96,2048]{2,1,0:T(8,128)(2,1)}, bf16[1,96,2048]{2,1,0:T(8,128)(2,1)S(1)}, u32[]{:S(2)}, u32[]{:S(2)}) collective-permute-start(bf16[1,96,2048]{2,1,0:T(8,128)(2,1)} %get-tuple-element.31), channel_id=1, source_target_pairs={{0,4},{1,5},{2,6},{3,7},{4,0},{5,1},{6,2},{7,3},{8,12},{9,13},{10,... | collective-permute-start | bytes 1179656 | tf_op jit(solution)/shard_map/ppermute | solution.py:18
  48.6 47.1 %collective-permute-start.4 = (bf16[1,96,2048]{2,1,0:T(8,128)(2,1)}, bf16[1,96,2048]{2,1,0:T(8,128)(2,1)S(1)}, u32[]{:S(2)}, u32[]{:S(2)}) collective-permute-start(bf16[1,96,2048]{2,1,0:T(8,128)(2,1)} %get-tuple-element.30), channel_id=1, source_target_pairs={{0,5},{1,4},{2,7},{3,6},{4,1},{5,0},{6,3},{7,2},{8,13},{9,12},{10,... | collective-permute-start | bytes 1179656 | tf_op jit(solution)/shard_map/ppermute | solution.py:18
  48.7 150.4 %reduce-scatter.2.cloned.1.call-start = ((), (), s32[]{:S(2)}) async-start(), calls=%async_computation.5 | async-start | bytes 3932160 | tf_op jit(solution)/shard_map/reduce_scatter | solution.py:117
  49.1 55.5 %collective-permute-start.5 = (bf16[1,96,2048]{2,1,0:T(8,128)(2,1)S(1)}, bf16[1,96,2048]{2,1,0:T(8,128)(2,1)S(1)}, u32[]{:S(2)}, u32[]{:S(2)}) collective-permute-start(bf16[1,96,2048]{2,1,0:T(8,128)(2,1)S(1)} %get-tuple-element.29), channel_id=1, source_target_pairs={{0,6},{1,7},{2,4},{3,5},{4,2},{5,3},{6,0},{7,1},{8,14},{9,15},{10,... | collective-permute-start | bytes 1179656 | tf_op jit(solution)/shard_map/ppermute | solution.py:18
  86.8 25.1 %collective-permute-start.6 = (bf16[1,96,2048]{2,1,0:T(8,128)(2,1)S(1)}, bf16[1,96,2048]{2,1,0:T(8,128)(2,1)S(1)}, u32[]{:S(2)}, u32[]{:S(2)}) collective-permute-start(bf16[1,96,2048]{2,1,0:T(8,128)(2,1)S(1)} %get-tuple-element.28), channel_id=1, source_target_pairs={{0,7},{1,6},{2,5},{3,4},{4,3},{5,2},{6,1},{7,0},{8,15},{9,14},{10,... | collective-permute-start | bytes 1179656 | tf_op jit(solution)/shard_map/ppermute | solution.py:18
  123.1 3.5 %copy-start.3 = (bf16[768,2048]{1,0:T(8,128)(2,1)S(1)}, bf16[768,2048]{1,0:T(8,128)(2,1)}, u32[]{:S(2)}) copy-start(bf16[768,2048]{1,0:T(8,128)(2,1)} %fusion) | copy-start | bytes 9437188
  126.7 1.1 copy-start.6
  135.4 1.0 copy-start.7
  136.4 7.4 %copy-start.4 = (bf16[1,2048,256]{2,1,0:T(8,128)(2,1)S(1)}, bf16[1,2048,256]{2,1,0:T(8,128)(2,1)}, u32[]{:S(2)}) copy-start(bf16[1,2048,256]{2,1,0:T(8,128)(2,1)} %all-gather.11.cloned.1.call-done) | copy-start | bytes 3145732
  140.5 7.9 %all-to-all-start.3 = ((bf16[8,1,96]{2,1,0:T(2,128)(2,1)}), bf16[8,1,96]{2,1,0:T(2,128)(2,1)S(1)}, u32[]{:S(2)}, u32[]{:S(2)}) async-start(bf16[8,1,96]{2,1,0:T(2,128)(2,1)} %convert_element_type.107), calls=%async_computation.3 | async-start | bytes 8192 | tf_op jit(solution)/shard_map/all_to_all | solution.py:131
  143.8 1.2 copy-start.5
  148.3 42.3 %all-to-all-start.2 = ((bf16[8,96,2048]{2,1,0:T(8,128)(2,1)}), bf16[8,96,2048]{2,1,0:T(8,128)(2,1)}, u32[]{:S(2)}, u32[]{:S(2)}) async-start(bf16[8,96,2048]{2,1,0:T(8,128)(2,1)} %bitcast.68), calls=%async_computation.2 | async-start | bytes 6291456 | tf_op jit(solution)/shard_map/all_to_all | solution.py:124
Sparse Core Ops, SparseCore 0:
  9.6 30.6 all-gather.10
  41.9 27.3 all-gather.8
  70.8 27.3 all-gather.6
  135.5 59.9 reduce-scatter.1
